TPU v7x, 32 devices: a whole 2x2x4 slice. The times are simulated.
32 devices in a mesh: groups: 2 (over y), wide: 8 (over z, x), narrow: 2 (over core).
Axes of the slice: x: 2, y: 2, z: 4, core: 2. Of those that a mesh axis runs over, the one named last changes fastest.
Arguments:
- states: bfloat16 [2048, 32, 256], P(None, ('groups', 'wide', 'narrow')), parts along dimension 1, may hold values from -6 to 6
- var_weights: bfloat16 [4, 256, 256], replicated, may hold values from -0.375 to 0.375
- samp_weights: bfloat16 [4, 256, 256], replicated, may hold values from -0.375 to 0.375
- norm_gains: float32 [3, 256], replicated, may hold values from 0.25 to 1.75
- edge_weights: bfloat16 [2, 256, 256], replicated, may hold values from -0.375 to 0.375
- none_weight: bfloat16 [256], replicated, may hold values from -0.375 to 0.375
Outputs:
- edge_prob: float32 [6, 2048, 2048], P('groups', 'wide', 'narrow'), parts along dimension 0
There are 2 independent parts, one for each index of `groups`. A program takes and returns all parts, laid end to end along the dimension named above; an argument that names none is the same for every part. Nothing has to cross between parts.
All inputs are finite; a program needn't handle non-finite values.
Results may differ from a plain program's by a relative error of at most 0.015.
The roundings to bfloat16 on the way count: a program that leaves them out, or rounds other values in their place, can miss the bound.
Values may be sent and summed in bfloat16 or wider, within the bound.
A program may use at most 64 MiB of HBM per device.

v0:
```python
import jax
import jax.numpy as jnp
from jax import lax
from jax.sharding import PartitionSpec as P

HEADS = 8


def layer_norm(values, gain):
    mean = jnp.mean(values, axis=-1, keepdims=True)
    centered = values - mean
    var = jnp.mean(centered * centered, axis=-1, keepdims=True)
    return centered * lax.rsqrt(var + 1e-05) * gain


def project(normed, weight):
    return jnp.dot(normed, weight, preferred_element_type=jnp.float32).astype(jnp.bfloat16)


def attend(seqs, gain, weights):
    batch, length, width = seqs.shape
    block = min(128, length)
    count = length // block
    normed = layer_norm(seqs.astype(jnp.float32), gain).astype(jnp.bfloat16)
    queries = project(normed, weights[0]).reshape(batch, length, HEADS, -1)
    keys_all = project(normed, weights[1]).reshape(batch, length, HEADS, -1)
    values_all = project(normed, weights[2]).reshape(batch, length, HEADS, -1)
    head_size = queries.shape[3]
    scale = 1.0 / head_size**0.5
    blocked = jnp.moveaxis(queries.reshape(batch, count, block, HEADS, head_size), 1, 0)

    def one_block(query_rows):
        scores = (
            jnp.einsum("bqhd,bkhd->bhqk", query_rows, keys_all, preferred_element_type=jnp.float32)
            * scale
        )
        expd = jnp.exp(scores)
        probs = (expd / jnp.sum(expd, axis=3, keepdims=True)).astype(jnp.bfloat16)
        return jnp.einsum(
            "bhqk,bkhd->bqhd", probs, values_all, preferred_element_type=jnp.float32
        ).astype(jnp.bfloat16)

    mixed = lax.map(one_block, blocked)
    joined = jnp.moveaxis(mixed, 0, 1).reshape(batch, length, width)
    update = jnp.dot(joined, weights[3], preferred_element_type=jnp.float32)
    return (seqs.astype(jnp.float32) + update).astype(jnp.bfloat16)


def edge_inputs(pooled, gain, edge_weights, none_weight):
    normed = layer_norm(pooled.astype(jnp.float32), gain).astype(jnp.bfloat16)
    source = project(normed, edge_weights[0])
    target = project(normed, edge_weights[1])
    none_term = jnp.dot(normed, none_weight, preferred_element_type=jnp.float32).astype(
        jnp.bfloat16
    )
    return (source, target, none_term)


def on_device(states, var_weights, samp_weights, norm_gains, edge_weights, none_weight):
    total_vars, samp_local, width = states.shape
    wide_count = lax.axis_size("wide")
    narrow_count = lax.axis_size("narrow")
    row_count = total_vars // wide_count
    col_count = total_vars // narrow_count
    by_sample = jnp.transpose(states, (1, 0, 2))
    mixed_var = attend(by_sample, norm_gains[0], var_weights)
    by_variable = jnp.transpose(mixed_var, (1, 0, 2))
    arranged = by_variable.reshape(wide_count, narrow_count, -1, samp_local, width)
    regrouped = lax.all_to_all(
        lax.all_to_all(arranged, "wide", split_axis=0, concat_axis=3, tiled=True),
        "narrow",
        split_axis=1,
        concat_axis=3,
        tiled=True,
    )
    per_variable = regrouped.reshape(regrouped.shape[2], regrouped.shape[3], width)
    mixed_samp = attend(per_variable, norm_gains[1], samp_weights)
    pooled = jnp.max(mixed_samp, axis=1)
    source, target, none_term = edge_inputs(pooled, norm_gains[2], edge_weights, none_weight)
    source_all, target_all, none_all = (
        lax.all_gather(source, ("wide", "narrow"), axis=0, tiled=True),
        lax.all_gather(target, ("wide", "narrow"), axis=0, tiled=True),
        lax.all_gather(none_term, ("wide", "narrow"), axis=0, tiled=True),
    )
    row_start = lax.axis_index("wide") * row_count
    col_start = lax.axis_index("narrow") * col_count
    source_rows = lax.dynamic_slice_in_dim(source_all, row_start, row_count, 0)
    target_rows = lax.dynamic_slice_in_dim(target_all, row_start, row_count, 0)
    none_rows = lax.dynamic_slice_in_dim(none_all, row_start, row_count, 0)
    source_cols = lax.dynamic_slice_in_dim(source_all, col_start, col_count, 0)
    target_cols = lax.dynamic_slice_in_dim(target_all, col_start, col_count, 0)
    none_cols = lax.dynamic_slice_in_dim(none_all, col_start, col_count, 0)
    escale = 1.0 / width**0.5
    forward = jnp.dot(source_rows, target_cols.T, preferred_element_type=jnp.float32) * escale
    backward = jnp.dot(target_rows, source_cols.T, preferred_element_type=jnp.float32) * escale
    absent = none_rows.astype(jnp.float32)[:, None] + none_cols.astype(jnp.float32)[None, :]
    expd = jnp.exp(jnp.stack([forward, backward, absent]))
    return expd / jnp.sum(expd, axis=0, keepdims=True)


def solution(mesh):
    return jax.shard_map(
        on_device,
        mesh=mesh,
        in_specs=(P(None, ("groups", "wide", "narrow"), None), P(), P(), P(), P(), P()),
        out_specs=P("groups", "wide", "narrow"),
        check_vma=False,
    )
```

profile of v0, /device:TPU:1, one launch (start us, length us, event | category | flops | bytes accessed | tf_op | source)
XLA Modules:
  0.0 282.6 jit_solution(10259456898689678925)
XLA Ops:
  6.5 1.7 convert_reduce_fusion
  8.2 1.9 fusion.18
  10.9 3.0 %convolution_convert_fusion.2 = bf16[2048,256]{1,0:T(8,128)(2,1)} fusion(bf16[4,256,256]{2,1,0:T(8,128)(2,1)} %param.9, bf16[2048,1,256]{2,0,1:T(8,128)(2,1)} %param.8, f32[256]{0:T(256)S(1)} %bitcast.181, f32[2048]{0:T(1024)S(1)} %add_rsqrt_fusion.1, f32[2048]{0:T(1024)S(1)} %broadcast_multiply_fusion.1), kind=kOutput, calls=%fused_computation.24 | convolution fusion | flops 271581184 | bytes 2245632 | tf_op jit(solution)/shard_map/dot_general | solution.py:17
  13.9 1.3 convolution_convert_fusion.1
  15.2 2.1 convolution_convert_fusion
  17.3 1.5 copy.56
  19.3 65.8 %while.2 = (s32[]{:T(128)}, bf16[16,1,128,8,32]{2,4,3,1,0:T(8,128)(2,1)}, bf16[16,1,128,8,32]{2,4,3,1,0:T(8,128)(2,1)S(1)}, bf16[1,2048,8,32]{1,3,2,0:T(8,128)(2...) while((s32[]{:T(128)}, bf16[16,1,128,8,32]{2,4,3,1,0:T(8,128)(2,1)}, ...), condition=%wide.region_4.5_spmd, body=%wide.region_2.4_spmd.sunk | while | flops 278952960 | bytes 23208548 | solution.py:43
  19.3 1.6 fusion.88
  20.9 2.5 fusion.89
  23.4 1.6 fusion.88
  25.0 2.5 fusion.89
  27.6 1.6 fusion.88
  29.1 2.5 fusion.89
  31.7 1.6 fusion.88
  33.3 2.5 fusion.89
  35.8 1.6 fusion.88
  37.4 2.5 fusion.89
  39.9 1.6 fusion.88
  41.5 2.5 fusion.89
  44.0 1.6 fusion.88
  45.6 2.5 fusion.89
  48.1 1.6 fusion.88
  49.7 2.5 fusion.89
  52.2 1.6 fusion.88
  53.8 2.5 fusion.89
  56.3 1.6 fusion.88
  57.9 2.5 fusion.89
  60.4 1.6 fusion.88
  62.0 2.5 fusion.89
  64.5 1.6 fusion.88
  66.1 2.5 fusion.89
  68.7 1.6 fusion.88
  70.2 2.5 fusion.89
  72.8 1.6 fusion.88
  74.4 2.5 fusion.89
  76.9 1.6 fusion.88
  78.5 2.5 fusion.89
  81.0 1.6 fusion.88
  82.6 2.5 fusion.89
  85.1 1.9 copy.58
  87.0 1.5 fusion.12
  88.5 31.0 %all_to_all.27 = bf16[8,2,128,1,256]{4,2,1,3,0:T(8,128)(2,1)S(1)} all-to-all(bf16[8,2,128,1,256]{4,2,1,3,0:T(8,128)(2,1)S(1)} %bitcast.174), channel_id=1, replica_groups=mesh['groups'=2,'wide'=8,'narrow'=2] {'wide'}, dimensions={0} | all-to-all | bytes 2097152 | tf_op jit(solution)/shard_map/all_to_all | solution.py:70
  119.6 6.2 %all_to_all.28 = bf16[1,2,128,8,256]{4,2,3,0,1:T(8,128)(2,1)S(1)} all-to-all(bf16[1,2,128,8,256]{4,2,3,0,1:T(8,128)(2,1)S(1)} %copy.60), channel_id=1, replica_groups=mesh['groups'=2,'wide'=8,'narrow'=2] {'narrow'}, dimensions={1} | all-to-all | bytes 2097152 | tf_op jit(solution)/shard_map/all_to_all | solution.py:69
  127.6 1.4 convolution_convert_fusion.4
  129.0 1.4 convolution_convert_fusion.3
  130.8 1.6 copy.62
  132.5 6.4 %copy.64 = bf16[128,16,8,32]{3,1,2,0:T(8,128)(2,1)} copy(bf16[128,16,8,32]{0,3,2,1:T(8,128)(2,1)S(1)} %bitcast.166) | data formatting | bytes 2097152 | tf_op jit(solution)/shard_map/while/body/jit(dynamic_index_in_dim)/squeeze | solution.py:43
  138.8 1.6 copy.63
  140.5 6.4 %copy.65 = bf16[128,16,8,32]{3,1,2,0:T(8,128)(2,1)} copy(bf16[128,16,8,32]{0,3,2,1:T(8,128)(2,1)S(1)} %bitcast.167) | data formatting | bytes 2097152 | tf_op jit(solution)/shard_map/reshape | solution.py:26
  146.9 9.0 %fusion.74 = f32[128,8,16,16]{2,3,1,0:T(8,128)} fusion(bf16[128,16,8,32]{3,1,2,0:T(8,128)(2,1)} %copy.64, bf16[128,16,8,32]{3,1,2,0:T(8,128)(2,1)} %copy.65), kind=kOutput, calls=%fused_computation.104 | convolution fusion | flops 16777216 | bytes 3145728 | tf_op jit(solution)/shard_map/while/body/eval_jaxpr/bqhd,bkhd->bhqk/dot_general | solution.py:34
  155.9 6.8 %copy.66 = f32[128,8,16,16]{0,3,2,1:T(8,128)S(1)} copy(f32[128,8,16,16]{2,3,1,0:T(8,128)} %fusion.74) | data formatting | bytes 2097152 | tf_op jit(solution)/shard_map/while/body/eval_jaxpr/bqhd,bkhd->bhqk/dot_general | solution.py:34
  162.9 1.0 divide_convert_fusion.8
  164.0 7.3 %copy.68 = bf16[128,8,16,16]{3,2,1,0:T(8,128)(2,1)} copy(bf16[128,8,16,16]{0,3,2,1:T(8,128)(2,1)} %divide_convert_fusion.8) | data formatting | bytes 1048576 | tf_op jit(solution)/shard_map/while/body/eval_jaxpr/convert_element_type | solution.py:38
  171.9 6.4 %copy.67 = bf16[128,16,8,32]{3,1,2,0:T(8,128)(2,1)} copy(bf16[128,16,8,32]{0,3,2,1:T(8,128)(2,1)S(1)} %bitcast.168) | data formatting | bytes 2097152 | tf_op jit(solution)/shard_map/reshape | solution.py:27
  178.3 7.8 %convert_bitcast_fusion = bf16[128,16,8,32]{3,1,2,0:T(8,128)(2,1)} fusion(bf16[128,8,16,16]{3,2,1,0:T(8,128)(2,1)} %copy.68, bf16[128,16,8,32]{3,1,2,0:T(8,128)(2,1)} %copy.67), kind=kOutput, calls=%fused_computation.14 | convolution fusion | flops 17301504 | bytes 2621440 | tf_op jit(solution)/shard_map/while/body/eval_jaxpr/bhqk,bkhd->bqhd/dot_general | solution.py:39
  186.1 5.5 %copy.69 = bf16[128,16,8,32]{0,3,2,1:T(8,128)(2,1)S(1)} copy(bf16[128,16,8,32]{3,1,2,0:T(8,128)(2,1)} %convert_bitcast_fusion) | data formatting | bytes 2097152 | tf_op jit(solution)/shard_map/while/body/eval_jaxpr/convert_element_type | solution.py:41
  191.5 1.4 fusion.29
  194.2 0.9 convolution_convert_fusion.7
  195.3 19.6 %all-gather = bf16[16,1,128]{2,1,0:T(2,128)(2,1)S(1)} all-gather(bf16[1,1,128]{2,1,0:T(2,128)(2,1)S(1)} %fusion.31), channel_id=1, replica_groups=mesh['groups'=2,'wide'=8,'narrow'=2] {'wide','narrow'}, dimensions={0}, use_global_device_ids=true | all-gather | bytes 4352 | tf_op jit(solution)/shard_map/all_gather | solution.py:83
  215.1 16.1 %all-gather.6.cloned.1.call-done = bf16[2048,256]{1,0:T(8,128)(2,1)} async-done(((bf16[128,256]{1,0:T(8,128)(2,1)}), bf16[2048,256]{1,0:T(8,128)(2,1)}) %all-gather.6.cloned.1.call-update) | async-done | bytes 1048592 | tf_op jit(solution)/shard_map/all_gather | solution.py:82
  231.2 39.0 %all-gather.4.cloned.1.call-done = bf16[2048,256]{1,0:T(8,128)(2,1)} async-done(((bf16[128,256]{1,0:T(8,128)(2,1)}), bf16[2048,256]{1,0:T(8,128)(2,1)}) %all-gather.4.cloned.1.call-update) | async-done | bytes 1048592 | tf_op jit(solution)/shard_map/all_gather | solution.py:81
  270.2 1.4 fusion.28
  271.7 1.5 fusion.27
  273.6 2.2 fusion.25
  (73 shorter events, 6.7 us)
Async XLA Ops:
  6.5 7.4 %copy-start = (bf16[2048,1,256]{2,0,1:T(8,128)(2,1)S(1)}, bf16[2048,1,256]{2,0,1:T(8,128)(2,1)}, u32[]{:S(2)}) copy-start(bf16[2048,1,256]{2,0,1:T(8,128)(2,1)} %param.8) | copy-start | bytes 3145732
  6.5 7.4 %copy-start.2 = (bf16[4,256,256]{2,1,0:T(8,128)(2,1)S(1)}, bf16[4,256,256]{2,1,0:T(8,128)(2,1)}, u32[]{:S(2)}) copy-start(bf16[4,256,256]{2,1,0:T(8,128)(2,1)} %param.9) | copy-start | bytes 1572868
  6.5 224.6 %all-gather.6.cloned.1.call-start = ((), (), s32[]{:S(2)}) async-start(), calls=%async_computation.3 | async-start | bytes 1114112 | tf_op jit(solution)/shard_map/all_gather | solution.py:82
  19.3 1.6 copy-start.5
  23.4 1.6 copy-start.5
  27.6 1.6 copy-start.5
  31.7 1.6 copy-start.5
  35.8 1.6 copy-start.5
  39.9 1.6 copy-start.5
  44.0 1.6 copy-start.5
  48.1 1.6 copy-start.5
  52.2 1.6 copy-start.5
  56.3 1.6 copy-start.5
  60.4 1.6 copy-start.5
  64.5 1.6 copy-start.5
  68.7 1.6 copy-start.5
  72.8 1.6 copy-start.5
  76.9 1.6 copy-start.5
  81.0 1.6 copy-start.5
  119.6 8.0 %copy-start.1 = (bf16[4,256,256]{2,1,0:T(8,128)(2,1)S(1)}, bf16[4,256,256]{2,1,0:T(8,128)(2,1)}, u32[]{:S(2)}) copy-start(bf16[4,256,256]{2,1,0:T(8,128)(2,1)} %param.10) | copy-start | bytes 1572868
  186.1 7.2 %copy-start.3 = (bf16[2,256,256]{2,1,0:T(8,128)(2,1)S(1)}, bf16[2,256,256]{2,1,0:T(8,128)(2,1)}, u32[]{:S(2)}) copy-start(bf16[2,256,256]{2,1,0:T(8,128)(2,1)} %param.12) | copy-start | bytes 786436
  186.1 9.0 %copy-start.4 = (bf16[256]{0:T(256)(128)(2,1)S(1)}, bf16[256]{0:T(256)(128)(2,1)}, u32[]{:S(2)}) copy-start(bf16[256]{0:T(256)(128)(2,1)} %param.13) | copy-start | bytes 1540
  194.1 76.1 %all-gather.4.cloned.1.call-start = ((), (), s32[]{:S(2)}) async-start(), calls=%async_computation.2 | async-start | bytes 1114112 | tf_op jit(solution)/shard_map/all_gather | solution.py:81
Sparse Core Ops, SparseCore 0:
  194.3 36.8 all-gather.5
  233.3 36.8 all-gather.3
where the time goes:
time: 284 us; the launch traced here: 283 us
  matrix products  99.6 us (35%)
  blocking collectives  56.8 us (20%)
  waiting for transfers between devices  55.1 us (19%)
  local copies, waits for them, and re-layouts  47.5 us (17%)
  between operations  13.7 us (5%)
  other arithmetic  9.79 us (3%)
    dot_general x17, matrix products, one_block(): jnp.einsum('bhqk,bkhd->bqhd', probs, values_all, preferred_element_type=j...  48 us
    all_gather x1, waiting for transfers between devices, on_device(): lax.all_gather(source, ('wide', 'narrow'), axis=0, tiled=True)  39 us
    dot_general x17, matrix products, one_block(): jnp.einsum('bqhd,bkhd->bhqk', query_rows, keys_all, preferred_element_typ...  34.3 us
    all_to_all x1, blocking collectives, on_device(): lax.all_to_all(arranged, 'wide', split_axis=0, concat_axis=3, tiled=True)  31 us
    all_gather x1, blocking collectives, on_device(): lax.all_gather(none_term, ('wide', 'narrow'), axis=0, tiled=True)  19.6 us
    all_gather x1, waiting for transfers between devices, on_device(): lax.all_gather(target, ('wide', 'narrow'), axis=0, tiled=True)  16.1 us
    dot_general x8, matrix products, project(): jnp.dot(normed, weight, preferred_element_type=jnp.float32)  11.3 us
    convert_element_type x1, local copies, waits for them, and re-layouts, one_block(): probs = (expd / jnp.sum(expd, axis=3, keepdims=True)).astype(jnp.bfloat16)  7.29 us
  transfers between devices with their start and end apart: 2, of which 2 were waited for; matrix products, arithmetic and copies ran while one was open for 0% of the time, Pallas kernels for 0%

commit v1 on v0

v1 whole, which is shorter than its diff:
```python
import functools
import math

import jax
import jax.numpy as jnp
from jax import lax
from jax.experimental import pallas as pl
from jax.experimental.pallas import tpu as pltpu
from jax.sharding import PartitionSpec as P

HEADS = 8
BLOCK = 128
KEYS = 256
F32, BF16 = jnp.float32, jnp.bfloat16
MESH = pl.DeviceIdType.MESH


def layer_norm(values, gain):
    mean = jnp.mean(values, axis=-1, keepdims=True)
    centered = values - mean
    var = jnp.mean(centered * centered, axis=-1, keepdims=True)
    return (centered * lax.rsqrt(var + 1e-05) * gain).astype(BF16)


def project(normed, weight):
    return jnp.dot(normed, weight, preferred_element_type=F32).astype(BF16)


def across(a, b):
    return lax.dot_general(a, b, (((1,), (1,)), ((), ())), preferred_element_type=F32)


def stack_heads(q, stacked):
    head = lax.broadcasted_iota(jnp.int32, q.shape, 1) // (q.shape[1] // HEADS)
    for h in range(HEADS):
        stacked[h * BLOCK : (h + 1) * BLOCK, :] = jnp.where(head == h, q, jnp.zeros_like(q))


def attend_block(stacked, keys_of, values_of, length, same):
    width = stacked.shape[1]
    step = min(KEYS, length)
    count = length // step
    factor = math.log2(math.e) / math.sqrt(width // HEADS)
    q = stacked[...]
    ahead = across(q, keys_of(0, step))
    acc = total = None
    for j in range(count):
        scores = ahead
        if j + 1 < count:
            ahead = across(q, keys_of((j + 1) * step, step))
        expd = jnp.exp2(scores * factor)
        if same is not None:
            expd = jnp.where(same, expd, 0.0)
        part = sum(expd[:, i : i + 128] for i in range(0, step, 128))
        total = part if total is None else total + part
        term = jnp.dot(expd.astype(BF16), values_of(j * step, step), preferred_element_type=F32)
        acc = term if acc is None else acc + term
    inverse = 4.0 / jnp.sum(total, axis=1, keepdims=True)
    acc = acc * inverse * 64.0
    head = lax.broadcasted_iota(jnp.int32, (BLOCK, width), 1) // (width // HEADS)
    out = acc[:BLOCK]
    for h in range(1, HEADS):
        out = jnp.where(head == h, acc[h * BLOCK : (h + 1) * BLOCK], out)
    return out.astype(BF16)


def mix_kernel(
    wide, narrow, x_ref, vw_ref, sw_ref, gain_ref, cols_ref, rows_ref,
    q_s, k_s, v_s, x_s, stacked, outbox, inbox, pooled, mine,
    send_a, recv_a, send_c, recv_c, send_r, recv_r,
):
    total_vars, width = x_ref.shape
    devices = wide * narrow
    own = total_vars // devices
    per_block = BLOCK // own
    blocks = total_vars // BLOCK
    my_wide, my_narrow = lax.axis_index("wide"), lax.axis_index("narrow")
    me = my_wide * narrow + my_narrow

    def device(d):
        return {"wide": d // narrow, "narrow": lax.rem(d, narrow)}

    barrier = pltpu.get_barrier_semaphore()

    def greet(d, carry):
        @pl.when(d != me)
        def _():
            pl.semaphore_signal(barrier, inc=1, device_id=device(d), device_id_type=MESH)

        return carry

    lax.fori_loop(0, devices, greet, 0)

    def keep(rows, normed, w_ref):
        q_s[rows, :] = project(normed, w_ref[0])
        k_s[rows, :] = project(normed, w_ref[1])
        v = project(normed, w_ref[2])
        v_s[rows, :] = (v.astype(F32) * 2.0**-8).astype(BF16)

    def prepare(i, carry):
        rows = pl.ds(pl.multiple_of(i * 256, 256), 256)
        keep(rows, layer_norm(x_ref[rows, :].astype(F32), gain_ref[0:1, :]), vw_ref)
        return carry

    lax.fori_loop(0, total_vars // 256, prepare, 0)

    my_block = me // per_block

    def post(block):
        def one(j, carry):
            d = block * per_block + j

            @pl.when(d != me)
            def _():
                pltpu.make_async_remote_copy(
                    src_ref=outbox.at[d], dst_ref=inbox.at[me],
                    send_sem=send_a.at[d], recv_sem=recv_a.at[me],
                    device_id=device(d), device_id_type=MESH,
                ).start()

            return carry

        lax.fori_loop(0, per_block, one, 0)

    def variable_block(t):
        block = lax.rem(my_block + 1 + t, blocks)
        rows = pl.ds(pl.multiple_of(block * BLOCK, BLOCK), BLOCK)
        stack_heads(q_s[rows, :], stacked.at[0])
        out = attend_block(
            stacked.at[0], lambda a, n: k_s[a : a + n, :], lambda a, n: v_s[a : a + n, :],
            total_vars, None,
        )
        update = jnp.dot(out, vw_ref[3], preferred_element_type=F32)
        mixed = x_ref[rows, :].astype(F32) + update
        outbox[pl.ds(block * per_block, per_block)] = mixed.reshape(per_block, own, width).astype(BF16)
        return block

    variable_block(0)
    pl.semaphore_wait(barrier, devices - 1)

    def variable_step(t, carry):
        post(lax.rem(my_block + t, blocks))
        variable_block(t)
        return carry

    lax.fori_loop(1, blocks, variable_step, 0)
    if per_block > 1:
        post(my_block)
    inbox[me] = outbox[me]

    def collect(d, carry):
        @pl.when(d != me)
        def _():
            pltpu.make_async_remote_copy(
                src_ref=outbox.at[d], dst_ref=inbox.at[d],
                send_sem=send_a.at[d], recv_sem=recv_a.at[d],
                device_id=device(d), device_id_type=MESH,
            ).wait()

        return carry

    lax.fori_loop(0, devices, collect, 0)

    tile = 8 * devices
    lump = 16 if own % 16 == 0 else 8

    def prepare_samples(i, carry):
        if lump == own:
            values = inbox[...].astype(F32)
        else:
            values = inbox[:, pl.ds(pl.multiple_of(i * lump, lump), lump), :].astype(F32)
        for half in range(lump // 8):
            start = (i * (lump // 8) + half) * tile
            rows = pl.ds(pl.multiple_of(start, tile), tile)
            tokens = values[:, half * 8 : half * 8 + 8, :].reshape(tile, width)
            x_s[rows, :] = tokens.astype(BF16)
            keep(rows, layer_norm(tokens, gain_ref[1:2, :]), sw_ref)
        return carry

    lax.fori_loop(0, own // lump, prepare_samples, 0)
    pooled[...] = jnp.full(pooled.shape, -jnp.inf, F32)
    step = min(KEYS, tile)
    row_var = lax.broadcasted_iota(jnp.int32, (HEADS * BLOCK, step), 0) % 8
    col_var = lax.broadcasted_iota(jnp.int32, (HEADS * BLOCK, step), 1) % 8
    same = row_var == col_var

    def sample_chunk(c, slot):
        rows = pl.ds(pl.multiple_of(c * BLOCK, BLOCK), BLOCK)
        base = c // (tile // BLOCK)
        stack_heads(q_s[rows, :], stacked.at[slot])

        def part(ref):
            return lambda a, n: ref[pl.ds(pl.multiple_of(base * tile + a, BLOCK), n), :]

        out = attend_block(stacked.at[slot], part(k_s), part(v_s), tile, same)
        update = jnp.dot(out, sw_ref[3], preferred_element_type=F32)
        mixed = (x_s[rows, :].astype(F32) + update).astype(BF16).astype(F32)
        best = jnp.max(mixed.reshape(BLOCK // 8, 8, width), axis=0)
        where = pl.ds(pl.multiple_of(base * 8, 8), 8)
        pooled[where, :] = jnp.maximum(pooled[where, :], best)

    piece = min(32, own)
    pieces = own // piece
    per_piece = piece * devices // BLOCK
    unroll = min(stacked.shape[0], per_piece)
    half = devices // narrow
    target = me // half
    slot = lax.rem(me, half)

    def to_cols(w, rows):
        return pltpu.make_async_remote_copy(
            src_ref=mine.at[rows], dst_ref=cols_ref.at[slot, rows],
            send_sem=send_c.at[w], recv_sem=recv_c.at[slot],
            device_id={"wide": w, "narrow": target}, device_id_type=MESH,
        )

    def to_rows(n, rows):
        return pltpu.make_async_remote_copy(
            src_ref=mine.at[rows], dst_ref=rows_ref.at[my_narrow, rows],
            send_sem=send_r.at[n], recv_sem=recv_r.at[my_narrow],
            device_id={"wide": my_wide, "narrow": n}, device_id_type=MESH,
        )

    def each_target(do, rows):
        def one(w, carry):
            @pl.when(w * narrow + target != me)
            def _():
                do(to_cols(w, rows))

            return carry

        lax.fori_loop(0, wide, one, 0)

        def other(n, carry):
            @pl.when(n != my_narrow)
            def _():
                do(to_rows(n, rows))

            return carry

        lax.fori_loop(0, narrow, other, 0)

    def piece_rows(g):
        return pl.ds(pl.multiple_of(g * piece, piece), piece)

    def sample_piece(g, carry):
        if pieces > 1:
            @pl.when(g > 0)
            def _():
                each_target(lambda copy: copy.start(), piece_rows(g - 1))

        def group(i, inner):
            for u in range(unroll):
                sample_chunk(g * per_piece + i * unroll + u, u)
            return inner

        if per_piece == unroll:
            group(0, 0)
        else:
            lax.fori_loop(0, per_piece // unroll, group, 0)
        rows = piece_rows(g)
        mine[rows, :] = layer_norm(pooled[rows, :], gain_ref[2:3, :])
        return carry

    lax.fori_loop(0, pieces, sample_piece, 0)
    each_target(lambda copy: copy.start(), piece_rows(pieces - 1))
    rows_ref[my_narrow] = mine[...]

    @pl.when(target == my_narrow)
    def _():
        cols_ref[slot] = mine[...]

    whole = pl.ds(0, own)
    each_target(lambda copy: copy.wait_send(), whole)

    def arrived(i, carry):
        @pl.when(my_narrow * half + i != me)
        def _():
            pltpu.make_async_remote_copy(
                src_ref=mine, dst_ref=cols_ref.at[i], send_sem=send_c.at[0],
                recv_sem=recv_c.at[i], device_id=device(me), device_id_type=MESH,
            ).wait_recv()

        return carry

    lax.fori_loop(0, half, arrived, 0)

    def beside(n, carry):
        @pl.when(n != my_narrow)
        def _():
            pltpu.make_async_remote_copy(
                src_ref=mine, dst_ref=rows_ref.at[n], send_sem=send_r.at[0],
                recv_sem=recv_r.at[n], device_id=device(me), device_id_type=MESH,
            ).wait_recv()

        return carry

    lax.fori_loop(0, narrow, beside, 0)


def edge_kernel(rows_ref, cols_ref, w_ref, none_ref, out_ref, src_s, dst_s, none_s):
    scale = 1.0 / rows_ref.shape[1] ** 0.5

    @pl.when(pl.program_id(0) == 0)
    def _():
        rows = rows_ref[...]
        src_s[...] = project(rows, w_ref[0])
        dst_s[...] = project(rows, w_ref[1])
        none_s[...] = across(rows, none_ref[...]).astype(BF16).astype(F32)

    cols = cols_ref[...]
    forward = jnp.exp(across(src_s[...], project(cols, w_ref[1])) * scale)
    backward = jnp.exp(across(dst_s[...], project(cols, w_ref[0])) * scale)
    none_cols = across(none_ref[...], cols).astype(BF16).astype(F32)
    absent = jnp.exp(none_s[:, 0:1] + none_cols[0:1, :])
    total = forward + backward + absent
    out_ref[0] = forward / total
    out_ref[1] = backward / total
    out_ref[2] = absent / total


def on_device(states, var_weights, samp_weights, norm_gains, edge_weights, none_weight):
    total_vars, samp_local, width = states.shape
    wide, narrow = lax.axis_size("wide"), lax.axis_size("narrow")
    devices = wide * narrow
    own = total_vars // devices
    assert samp_local == 1 and BLOCK % own == 0 and own % 8 == 0
    half = devices // narrow
    vmem = pl.BlockSpec(memory_space=pltpu.VMEM)
    dma = pltpu.SemaphoreType.DMA
    cols, rows = pl.pallas_call(
        functools.partial(mix_kernel, wide, narrow),
        out_shape=(
            jax.ShapeDtypeStruct((half, own, width), BF16),
            jax.ShapeDtypeStruct((narrow, own, width), BF16),
        ),
        in_specs=[vmem] * 4,
        out_specs=(vmem, vmem),
        scratch_shapes=[pltpu.VMEM((total_vars, width), BF16)] * 4
        + [
            pltpu.VMEM((4, HEADS * BLOCK, width), BF16),
            pltpu.VMEM((devices, own, width), BF16),
            pltpu.VMEM((devices, own, width), BF16),
            pltpu.VMEM((own, width), F32),
            pltpu.VMEM((own, width), BF16),
            dma((devices,)), dma((devices,)), dma((wide,)), dma((half,)),
            dma((narrow,)), dma((narrow,)),
        ],
        compiler_params=pltpu.CompilerParams(
            collective_id=0, has_side_effects=True, vmem_limit_bytes=60 * 2**20
        ),
        name="mix",
    )(states.reshape(total_vars, width), var_weights, samp_weights, norm_gains)
    cols = cols.reshape(half * own, width)
    rows = rows.reshape(narrow * own, width)
    row_count, col_count = narrow * own, half * own
    tile = min(256, col_count)
    none_rows = jnp.broadcast_to(none_weight[None, :], (16, width))
    return pl.pallas_call(
        edge_kernel,
        grid=(col_count // tile,),
        out_shape=jax.ShapeDtypeStruct((3, row_count, col_count), F32),
        in_specs=[
            pl.BlockSpec((row_count, width), lambda i: (0, 0)),
            pl.BlockSpec((tile, width), lambda i: (i, 0)),
            pl.BlockSpec((2, width, width), lambda i: (0, 0, 0)),
            pl.BlockSpec((16, width), lambda i: (0, 0)),
        ],
        out_specs=pl.BlockSpec((3, row_count, tile), lambda i: (0, 0, i)),
        scratch_shapes=[
            pltpu.VMEM((row_count, width), BF16),
            pltpu.VMEM((row_count, width), BF16),
            pltpu.VMEM((row_count, 16), F32),
        ],
        name="edge",
    )(rows, cols, edge_weights, none_rows)


def solution(mesh):
    return jax.shard_map(
        on_device,
        mesh=mesh,
        in_specs=(P(None, ("groups", "wide", "narrow"), None), P(), P(), P(), P(), P()),
        out_specs=P("groups", "wide", "narrow"),
        check_vma=False,
    )
```

time: 284 us -> 75.4 us (0.27)
  matrix products: 99.6 us -> 0 us
  Pallas kernels: 0 us -> 73.9 us
  blocking collectives: 56.8 us -> 0 us
  waiting for transfers between devices: 55.1 us -> 0 us
  local copies, waits for them, and re-layouts: 47.5 us -> 1.25 us
  between operations: 13.7 us -> 0.01 us
  other arithmetic: 9.79 us -> 0 us
    dot_general x47 -> x0, matrix products: 99.6 us -> none  [the longest x17 48 us: one_block(): jnp.einsum('bhqk,bkhd->bqhd', probs, values_all, preferred_element_type=j...]
    pallas_call x0 -> x2, Pallas kernels: none -> 73.9 us  [the longest x1 68.9 us: on_device(): pl.pallas_call(functools.partial(mix_kernel, wide, narrow), out_shape=(ja...]
    all_gather x2 -> x0, waiting for transfers between devices: 55.1 us -> none  [the longest x1 39 us: on_device(): lax.all_gather(source, ('wide', 'narrow'), axis=0, tiled=True)]
    all_to_all x2 -> x0, blocking collectives: 37.3 us -> none  [the longest x1 31 us: on_device(): lax.all_to_all(arranged, 'wide', split_axis=0, concat_axis=3, tiled=True)]
    all_gather x1 -> x0, blocking collectives: 19.6 us -> none  [on_device(): lax.all_gather(none_term, ('wide', 'narrow'), axis=0, tiled=True)]
    convert_element_type x6 -> x0, local copies, waits for them, and re-layouts: 18.1 us -> none  [the longest x1 7.29 us: one_block(): probs = (expd / jnp.sum(expd, axis=3, keepdims=True)).astype(jnp.bfloat16)]
    reshape x2 -> x0, local copies, waits for them, and re-layouts: 12.8 us -> none  [the longest x1 6.4 us: attend(): keys_all = project(normed, weights[1]).reshape(batch, length, HEADS, -1)]
    dot_general x1 -> x0, local copies, waits for them, and re-layouts: 6.76 us -> none  [one_block(): jnp.einsum('bqhd,bkhd->bhqk', query_rows, keys_all, preferred_element_typ...]
  transfers between devices with their start and end apart: 2 -> 0, of which waited for: 2 -> 0; matrix products, arithmetic and copies ran while one was open for 0% -> 0% of each run, Pallas kernels for 0% -> 0%
where the time goes in v1:
time: 75.4 us; the launch traced here: 75.1 us
  Pallas kernels  73.9 us (98%)
  local copies, waits for them, and re-layouts  1.25 us (2%)
    pallas_call x1, Pallas kernels, on_device(): pl.pallas_call(functools.partial(mix_kernel, wide, narrow), out_shape=(ja...  68.9 us
    pallas_call x1, Pallas kernels, on_device(): pl.pallas_call(edge_kernel, grid=(col_count // tile,), out_shape=jax.Shap...  5.01 us

profile of v1, /device:TPU:1, one launch (start us, length us, event | category | flops | bytes accessed | tf_op | source)
XLA Modules:
  0.0 75.1 jit_solution(17324300225338756996)
XLA Ops:
  0.0 1.3 %broadcast_in_dim.2.none_ref = bf16[16,256]{1,0:T(8,128)(2,1)} broadcast(bf16[256]{0:T(256)(128)(2,1)} %param.11), dimensions={1} | broadcast | bytes 8704 | tf_op jit(solution)/shard_map/broadcast_in_dim | solution.py:358
  1.3 68.9 %mix.1 = (bf16[8,128,256]{2,1,0:T(8,128)(2,1)}, bf16[2,128,256]{2,1,0:T(8,128)(2,1)}) custom-call(bf16[2048,256]{1,0:T(8,128)(2,1)} %bitcast.3, bf16[4,256,256]{2,1,0:T(8,128)(2,1)} %vw_ref.1, bf16[4,256,256]{2,1,0:T(8,128)(2,1)} %sw_ref.1, f32[3,256]{1,0:T(4,128)} %gain_ref.1), custom_call_target="tpu_custom_call" | custom-call | tf_op jit(solution)/shard_map/mix/pallas_call | solution.py:331
  70.1 5.0 %edge.1 = f32[3,256,1024]{2,1,0:T(8,128)} custom-call(bf16[256,256]{1,0:T(8,128)(2,1)} %bitcast.5, bf16[1024,256]{1,0:T(8,128)(2,1)} %bitcast.4, bf16[2,256,256]{2,1,0:T(8,128)(2,1)} %w_ref.1, bf16[16,256]{1,0:T(8,128)(2,1)} %broadcast_in_dim.2.none_ref), custom_call_target="tpu_custom_call" | custom-call | tf_op jit(solution)/shard_map/edge/pallas_call | solution.py:359

commit v2 on v1

--- a/solution.py
+++ b/solution.py
@@ -10,6 +10,7 @@
 
 HEADS = 8
 BLOCK = 128
+QUERIES = 256
 KEYS = 256
 F32, BF16 = jnp.float32, jnp.bfloat16
 MESH = pl.DeviceIdType.MESH
@@ -33,7 +34,7 @@
 def stack_heads(q, stacked):
     head = lax.broadcasted_iota(jnp.int32, q.shape, 1) // (q.shape[1] // HEADS)
     for h in range(HEADS):
-        stacked[h * BLOCK : (h + 1) * BLOCK, :] = jnp.where(head == h, q, jnp.zeros_like(q))
+        stacked[h * q.shape[0] : (h + 1) * q.shape[0], :] = jnp.where(head == h, q, jnp.zeros_like(q))
 
 
 def attend_block(stacked, keys_of, values_of, length, same):
@@ -64,16 +65,38 @@
     return out.astype(BF16)
 
 
+def attend_across(stacked, keys, values):
+    length, width = keys.shape
+    size = width // HEADS
+    step = min(KEYS, length)
+    factor = math.log2(math.e) / math.sqrt(size)
+    outs = []
+    for h in range(HEADS):
+        q = stacked[h * QUERIES : (h + 1) * QUERIES, :]
+        pieces, total = [], None
+        for j in range(0, length, step):
+            expd = jnp.exp2(across(keys[j : j + step, :], q) * factor)
+            part = jnp.sum(expd.reshape(step // 8, 8, QUERIES), axis=0)
+            total = part if total is None else total + part
+            pieces.append(expd.astype(BF16))
+        acc = jnp.dot(
+            values[h * size : (h + 1) * size, :], jnp.concatenate(pieces, axis=0),
+            preferred_element_type=F32,
+        )
+        outs.append(acc * (4.0 / jnp.sum(total, axis=0, keepdims=True)) * 64.0)
+    return jnp.transpose(jnp.concatenate(outs, axis=0)).astype(BF16)
+
+
 def mix_kernel(
     wide, narrow, x_ref, vw_ref, sw_ref, gain_ref, cols_ref, rows_ref,
-    q_s, k_s, v_s, x_s, stacked, outbox, inbox, pooled, mine,
+    q_s, k_s, v_s, x_s, vt_s, queries, stacked, outbox, inbox, pooled, mine,
     send_a, recv_a, send_c, recv_c, send_r, recv_r,
 ):
     total_vars, width = x_ref.shape
     devices = wide * narrow
     own = total_vars // devices
-    per_block = BLOCK // own
-    blocks = total_vars // BLOCK
+    per_block = QUERIES // own
+    blocks = total_vars // QUERIES
     my_wide, my_narrow = lax.axis_index("wide"), lax.axis_index("narrow")
     me = my_wide * narrow + my_narrow
 
@@ -94,12 +117,12 @@
     def keep(rows, normed, w_ref):
         q_s[rows, :] = project(normed, w_ref[0])
         k_s[rows, :] = project(normed, w_ref[1])
-        v = project(normed, w_ref[2])
-        v_s[rows, :] = (v.astype(F32) * 2.0**-8).astype(BF16)
+        return project(normed, w_ref[2]).astype(F32) * 2.0**-8
 
     def prepare(i, carry):
         rows = pl.ds(pl.multiple_of(i * 256, 256), 256)
-        keep(rows, layer_norm(x_ref[rows, :].astype(F32), gain_ref[0:1, :]), vw_ref)
+        v = keep(rows, layer_norm(x_ref[rows, :].astype(F32), gain_ref[0:1, :]), vw_ref)
+        vt_s[:, rows] = jnp.transpose(v).astype(BF16)
         return carry
 
     lax.fori_loop(0, total_vars // 256, prepare, 0)
@@ -124,12 +147,9 @@
 
     def variable_block(t):
         block = lax.rem(my_block + 1 + t, blocks)
-        rows = pl.ds(pl.multiple_of(block * BLOCK, BLOCK), BLOCK)
-        stack_heads(q_s[rows, :], stacked.at[0])
-        out = attend_block(
-            stacked.at[0], lambda a, n: k_s[a : a + n, :], lambda a, n: v_s[a : a + n, :],
-            total_vars, None,
-        )
+        rows = pl.ds(pl.multiple_of(block * QUERIES, QUERIES), QUERIES)
+        stack_heads(q_s[rows, :], queries)
+        out = attend_across(queries, k_s, vt_s)
         update = jnp.dot(out, vw_ref[3], preferred_element_type=F32)
         mixed = x_ref[rows, :].astype(F32) + update
         outbox[pl.ds(block * per_block, per_block)] = mixed.reshape(per_block, own, width).astype(BF16)
@@ -174,7 +194,8 @@
             rows = pl.ds(pl.multiple_of(start, tile), tile)
             tokens = values[:, half * 8 : half * 8 + 8, :].reshape(tile, width)
             x_s[rows, :] = tokens.astype(BF16)
-            keep(rows, layer_norm(tokens, gain_ref[1:2, :]), sw_ref)
+            v = keep(rows, layer_norm(tokens, gain_ref[1:2, :]), sw_ref)
+            v_s[rows, :] = v.astype(BF16)
         return carry
 
     lax.fori_loop(0, own // lump, prepare_samples, 0)
@@ -338,6 +359,8 @@
         out_specs=(vmem, vmem),
         scratch_shapes=[pltpu.VMEM((total_vars, width), BF16)] * 4
         + [
+            pltpu.VMEM((width, total_vars), BF16),
+            pltpu.VMEM((HEADS * QUERIES, width), BF16),
             pltpu.VMEM((4, HEADS * BLOCK, width), BF16),
             pltpu.VMEM((devices, own, width), BF16),
             pltpu.VMEM((devices, own, width), BF16),

time: 75.4 us -> 68 us (0.902)
  Pallas kernels: 73.9 us -> 66.6 us
    pallas_call x1, Pallas kernels: 68.9 us -> 61.5 us  [on_device(): pl.pallas_call(functools.partial(mix_kernel, wide, narrow), out_shape=(ja...]
where the time goes in v2:
time: 68 us; the launch traced here: 67.8 us
  Pallas kernels  66.6 us (98%)
  local copies, waits for them, and re-layouts  1.25 us (2%)
    pallas_call x1, Pallas kernels, on_device(): pl.pallas_call(functools.partial(mix_kernel, wide, narrow), out_shape=(ja...  61.5 us
    pallas_call x1, Pallas kernels, on_device(): pl.pallas_call(edge_kernel, grid=(col_count // tile,), out_shape=jax.Shap...  5.01 us

profile of v2, /device:TPU:1, one launch (start us, length us, event | category | flops | bytes accessed | tf_op | source)
XLA Modules:
  0.0 67.8 jit_solution(11850907436132946184)
XLA Ops:
  0.0 1.3 %broadcast_in_dim.2.none_ref = bf16[16,256]{1,0:T(8,128)(2,1)} broadcast(bf16[256]{0:T(256)(128)(2,1)} %param.11), dimensions={1} | broadcast | bytes 8704 | tf_op jit(solution)/shard_map/broadcast_in_dim | solution.py:381
  1.3 61.5 %mix.1 = (bf16[8,128,256]{2,1,0:T(8,128)(2,1)}, bf16[2,128,256]{2,1,0:T(8,128)(2,1)}) custom-call(bf16[2048,256]{1,0:T(8,128)(2,1)} %bitcast.3, bf16[4,256,256]{2,1,0:T(8,128)(2,1)} %vw_ref.1, bf16[4,256,256]{2,1,0:T(8,128)(2,1)} %sw_ref.1, f32[3,256]{1,0:T(4,128)} %gain_ref.1), custom_call_target="tpu_custom_call" | custom-call | tf_op jit(solution)/shard_map/mix/pallas_call | solution.py:352
  62.8 5.0 %edge.1 = f32[3,256,1024]{2,1,0:T(8,128)} custom-call(bf16[256,256]{1,0:T(8,128)(2,1)} %bitcast.5, bf16[1024,256]{1,0:T(8,128)(2,1)} %bitcast.4, bf16[2,256,256]{2,1,0:T(8,128)(2,1)} %w_ref.1, bf16[16,256]{1,0:T(8,128)(2,1)} %broadcast_in_dim.2.none_ref), custom_call_target="tpu_custom_call" | custom-call | tf_op jit(solution)/shard_map/edge/pallas_call | solution.py:382
